TPU v7x, 256 devices: a whole 4x4x8 slice. The times are simulated.
256 devices in a mesh: gx: 32 (over x, y, core), gy: 8 (over z).
Axes of the slice: x: 4, y: 4, z: 8, core: 2. Of those that a mesh axis runs over, the one named last changes fastest.
Arguments:
- hidden: bfloat16 [1024, 16384], P('gx', 'gy'), may hold values from -40 to 40
- lm_head: bfloat16 [16384, 65536], P('gy', 'gx'), may hold values from -1 to 1
- parent: int32 [1024], replicated, may hold values from 0 to 1023, as said below
- draft_token: int32 [1024], replicated, may hold values from 0 to 65535
- draft_prob: float32 [1024], replicated, may hold values from 0.01 to 1
- uniforms: float32 [1024], replicated, may hold values from 0.01 to 1
- node_count: int32 [16], replicated, may hold values from 1 to 64, as said below
- accepted_end: int32 [16], replicated, may hold values from 0 to 63, as said below
Outputs:
- vertex_accept_slack: float32 [1024], P('gx')
- lineage_least_slack: float32 [1024], P('gx')
- extra_draw_score: float32 [16, 65536], P(None, 'gx')
Inputs may be any that keep to these rules, and one draw needn't show every extreme that they name: A node's parent lies in the same sequence at a lower slot; slot 0 of each sequence is its own parent. `node_count`: some sequence has all 64 slots live. `accepted_end`: the slot of a live node of that sequence.
All inputs are finite; a program needn't handle non-finite values.
Results may differ from a plain program's by a relative error of at most 0.0003.
Values may be sent and summed in bfloat16 or wider, within the bound.
A program may use at most 64 MiB of HBM per device.

v0:
```python
import jax
import jax.numpy as jnp
from jax import lax
from jax.sharding import Mesh
from jax.sharding import PartitionSpec as P

GX = ("gx_0", "gx_1", "gx_2")
big_margin = 10000.0


def in_order(tiles, dim):
    shape = list(tiles.shape[1:])
    shape[dim] *= tiles.shape[0]
    return jnp.moveaxis(tiles, 0, dim).reshape(shape)


def all_blocks(x, axes, sequence):
    tiles = x[None]
    for k in sequence:
        tiles = lax.all_gather(tiles, axes[k], axis=0, tiled=True)
    held = [lax.axis_size(axes[k]) for k in reversed(sequence)]
    tiles = tiles.reshape(*held, *x.shape)
    turned = sorted(range(len(sequence)), key=lambda place: sequence[len(sequence) - 1 - place])
    return tiles.transpose(*turned, *range(len(sequence), tiles.ndim)).reshape(-1, *x.shape)


def whole_of(x, axes, sequence, dim):
    return in_order(all_blocks(x, axes, sequence), dim)


def from_everyone(x, axis):
    copies = jnp.broadcast_to(x, (lax.axis_size(axis), *x.shape))
    return lax.all_to_all(copies, axis, split_axis=0, concat_axis=0, tiled=True)


def all_in_one(x, axis):
    leaves = jax.tree.leaves(x)
    sequence = sorted(range(len(leaves)), key=lambda k: -leaves[k].size)
    width = (1, *leaves[sequence[0]].shape)[-1]
    lines = [
        jnp.pad(leaves[k].reshape(-1), (0, -leaves[k].size % width)).reshape(-1, width)
        for k in sequence
    ]
    both, at, found = (from_everyone(jnp.concatenate(lines), axis), 0, {})
    for k, line in zip(sequence, lines):
        section = both[:, at : at + len(line)].reshape(len(both), -1)
        found[k] = section[:, : leaves[k].size].reshape(-1, *leaves[k].shape)
        at += len(line)
    numbers = iter(range(len(leaves)))
    return jax.tree.map(lambda _: found[next(numbers)], x)


def joined_by_halves(pieces, combine):
    while len(jax.tree.leaves(pieces)[0]) > 1:
        pieces = jax.vmap(combine)(
            *(jax.tree.map(lambda part: part[side::2], pieces) for side in (0, 1))
        )
    return jax.tree.map(lambda part: part[0], pieces)


def combined_all(x, axis, combine):
    pieces = all_in_one(x, axis)
    return joined_by_halves(pieces, combine)


def taken_together(x, axis):
    return from_everyone(x, axis).sum(axis=0)


def together(arrays, axis):
    ends = [0]
    for a in arrays:
        ends.append(ends[-1] + a.size)
    subtotal = taken_together(jnp.concatenate([a.ravel() for a in arrays]), axis)
    return tuple((subtotal[b:e].reshape(a.shape) for a, b, e in zip(arrays, ends, ends[1:])))


def combine_stats(first, second):
    top = jnp.maximum(first[0], second[0])
    total = first[1] * jnp.exp(first[0] - top) + second[1] * jnp.exp(second[0] - top)
    return (top, total, first[2] + second[2])


def local(hidden, lm_head, parent, draft_token, draft_prob, uniforms, node_count, accepted_end):
    out_rows = hidden.shape[0]
    out_start = lax.axis_index(GX) * out_rows
    node_total = parent.shape[0]
    seq_total = node_count.shape[0]
    tree_size = node_total // seq_total
    width = lm_head.shape[1]
    vocab_base = lax.axis_index(GX) * width
    leaf_entries = jnp.arange(seq_total, dtype=jnp.int32) * tree_size + accepted_end
    columns = whole_of(hidden, GX, (1, 0, 2), 0)
    row_count = node_total // lax.axis_size("gy")
    start_row = lax.axis_index("gy") * row_count
    emitted_scores = lax.psum_scatter(
        jnp.dot(columns, lm_head, preferred_element_type=jnp.float32),
        "gy",
        scatter_dimension=0,
        tiled=True,
    )
    own_parent = parent - start_row
    own_token = draft_token - vocab_base
    hit_mask = (own_parent >= 0) & (own_parent < row_count) & (own_token >= 0) & (own_token < width)
    picked = emitted_scores[
        jnp.clip(own_parent, 0, row_count - 1), jnp.clip(own_token, 0, width - 1)
    ]
    target_part = jnp.where(hit_mask, picked, 0.0)
    local_max = jnp.max(emitted_scores, axis=1)
    local_sum = jnp.sum(jnp.exp(emitted_scores - local_max[:, None]), axis=1)
    row_max, row_sum, target_part = combined_all(
        (local_max, local_sum, target_part), GX, combine_stats
    )
    row_log_total = row_max + jnp.log(row_sum)
    total_part = lax.dynamic_update_slice_in_dim(
        jnp.zeros((node_total,), jnp.float32), row_log_total, start_row, 0
    )
    own_end = leaf_entries - start_row
    owned = (own_end >= 0) & (own_end < row_count)
    end_part = jnp.where(owned[:, None], emitted_scores[jnp.clip(own_end, 0, row_count - 1)], 0.0)
    partition_function, target, leaf_scores = together((total_part, target_part, end_part), "gy")
    extra_draw_score = leaf_scores - partition_function[leaf_entries][:, None]
    margin = target - partition_function[parent] - jnp.log(draft_prob) - jnp.log(uniforms)
    node_index = jnp.arange(node_total, dtype=jnp.int32)
    local_index = node_index % tree_size
    live_mask = local_index < node_count[node_index // tree_size]
    root_mask = parent == node_index
    spare_mask = jnp.logical_or(root_mask, jnp.logical_not(live_mask))
    all_margin = jnp.where(spare_mask, 0.0, margin)
    path_min = jnp.where(root_mask, big_margin, margin)
    ancestor = parent
    for _ in range((tree_size - 1).bit_length()):
        path_min = jnp.minimum(path_min, path_min[ancestor])
        ancestor = ancestor[ancestor]
    all_path = jnp.where(spare_mask, 0.0, path_min)
    vertex_accept_slack = lax.dynamic_slice_in_dim(all_margin, out_start, out_rows, 0)
    lineage_least_slack = lax.dynamic_slice_in_dim(all_path, out_start, out_rows, 0)
    return (vertex_accept_slack, lineage_least_slack, extra_draw_score)


def solution(mesh):
    finer = Mesh(mesh.devices.reshape(4, 4, 2, mesh.shape["gy"]), ("gx_0", "gx_1", "gx_2", "gy"))
    placed = (P(GX, "gy"), P("gy", GX), P(), P(), P(), P(), P(), P())
    return jax.shard_map(
        local, mesh=finer, in_specs=placed, out_specs=(P(GX), P(GX), P(None, GX)), check_vma=False
    )
```

profile of v0, /device:TPU:1, one launch (start us, length us, event | category | flops | bytes accessed | tf_op | source)
XLA Modules:
  0.0 307.7 jit_solution(15902408323733157968)
XLA Ops:
  7.2 13.3 %all-gather = bf16[128,2048]{1,0:T(8,128)(2,1)} all-gather(bf16[32,2048]{1,0:T(8,128)(2,1)} %param.8), channel_id=2, replica_groups=mesh['gx_0'=4,'gx_1'=4,'gx_2'=2,'gy'=8] {'gx_1'}, dimensions={0}, use_global_device_ids=true | all-gather | bytes 655360 | tf_op jit(solution)/shard_map/all_gather | solution.py:20
  20.6 37.3 %all-gather.4.cloned.1.call-done = bf16[16,32,2048]{2,1,0:T(8,128)(2,1)} async-done(((bf16[4,32,2048]{2,1,0:T(8,128)(2,1)}), bf16[16,32,2048]{2,1,0:T(8,128)(2,1)}) %all-gather.4.cloned.1.call-update) | async-done | bytes 2097168 | tf_op jit(solution)/shard_map/all_gather | solution.py:20
  57.9 21.7 %all-gather.6.cloned.1.call-done = bf16[32,32,2048]{2,1,0:T(8,128)(2,1)} async-done(((bf16[16,32,2048]{2,1,0:T(8,128)(2,1)}), bf16[32,32,2048]{2,1,0:T(8,128)(2,1)}) %all-gather.6.cloned.1.call-update) | async-done | bytes 4194320 | tf_op jit(solution)/shard_map/all_gather | solution.py:20
  79.6 2.7 copy.16
  82.3 2.0 copy-done.8
  84.3 11.0 %fusion.17 = f32[1024,2048]{1,0:T(8,128)} fusion(bf16[1024,2048]{1,0:T(8,128)(2,1)S(1)} %bitcast.55, bf16[2048,2048]{1,0:T(8,128)(2,1)S(1)} %copy-done.8), kind=kOutput, calls=%fused_computation.94 | convolution fusion | flops 8589934592 | bytes 20971520 | tf_op jit(solution)/shard_map/dot_general | solution.py:97
  96.0 4.5 %gather_fusion.4 = s32[1024]{0:T(1024)S(1)} fusion(s32[1024]{0:T(1024)S(1)} %copy-done, s32[1024]{0:T(1024)S(1)} %get-tuple-element.19), kind=kCustom, calls=%fused_computation.4 | custom fusion | bytes 12288 | tf_op jit(solution)/shard_map/gather | solution.py:134
  100.6 90.3 %reduce-scatter.2.cloned.1.call-done = f32[128,2048]{1,0:T(8,128)} async-done(((f32[1024,2048]{1,0:T(8,128)}), f32[128,2048]{1,0:T(8,128)}) %reduce-scatter.2.cloned.1.call-update) | async-done | bytes 1048592 | tf_op jit(solution)/shard_map/reduce_scatter | solution.py:96
  190.9 1.4 reduce_max.9
  192.3 1.5 exponential_reduce_fusion
  193.9 8.6 %gather_fusion = f32[1024]{0:T(1024)S(1)} fusion(f32[128,2048]{1,0:T(8,128)S(1)} %copy-done.1, s32[1024]{0:T(1024)S(1)} %get-tuple-element.20), kind=kCustom, calls=%fused_computation | custom fusion | bytes 16384 | tf_op jit(solution)/shard_map/gather | solution.py:105
  202.5 0.9 broadcast_in_dim.66
  203.4 7.6 %all-to-all-start = ((f32[32,3,1024]{2,1,0:T(4,128)}), f32[32,3,1024]{2,1,0:T(4,128)S(1)}, u32[]{:S(2)}, u32[]{:S(2)}) async-start(f32[32,3,1024]{2,1,0:T(4,128)} %broadcast_in_dim.66), calls=%async_computation.1 | async-start | bytes 1048576 | tf_op jit(solution)/shard_map/all_to_all | solution.py:33
  211.0 4.5 %gather_fusion.6 = s32[1024]{0:T(1024)S(1)} fusion(s32[1024]{0:T(1024)S(1)} %gather_fusion.4, s32[1024]{0:T(1024)S(1)} %broadcast_clamp_fusion.4), kind=kCustom, calls=%fused_computation.6 | custom fusion | bytes 12288 | tf_op jit(solution)/shard_map/gather | solution.py:134
  216.3 6.3 %all-to-all-done = f32[32,3,1024]{2,1,0:T(4,128)S(1)} async-done(((f32[32,3,1024]{2,1,0:T(4,128)}), f32[32,3,1024]{2,1,0:T(4,128)S(1)}, u32[]{:S(2)}, u32[]{:S(2)}) %all-to-all-start) | async-done | bytes 393248 | tf_op jit(solution)/shard_map/all_to_all | solution.py:33
  223.8 1.6 broadcast_in_dim.70
  225.4 4.1 %all-to-all-start.1 = ((f32[8,1,34816]{2,1,0:T(1,128)}), f32[8,1,34816]{2,1,0:T(1,128)S(1)}, u32[]{:S(2)}, u32[]{:S(2)}) async-start(f32[8,1,34816]{2,1,0:T(1,128)} %broadcast_in_dim.70), calls=%async_computation.2 | async-start | bytes 2228224 | tf_op jit(solution)/shard_map/all_to_all | solution.py:33
  229.5 4.5 %gather_fusion.8 = s32[1024]{0:T(1024)S(1)} fusion(s32[1024]{0:T(1024)S(1)} %gather_fusion.6, s32[1024]{0:T(1024)S(1)} %broadcast_clamp_fusion.3), kind=kCustom, calls=%fused_computation.8 | custom fusion | bytes 12288 | tf_op jit(solution)/shard_map/gather | solution.py:134
  234.0 4.5 %gather_fusion.10 = s32[1024]{0:T(1024)S(1)} fusion(s32[1024]{0:T(1024)S(1)} %gather_fusion.8, s32[1024]{0:T(1024)S(1)} %broadcast_clamp_fusion.2), kind=kCustom, calls=%fused_computation.10 | custom fusion | bytes 12288 | tf_op jit(solution)/shard_map/gather | solution.py:134
  238.6 4.5 %gather_fusion.12 = s32[1024]{0:T(1024)S(1)} fusion(s32[1024]{0:T(1024)S(1)} %gather_fusion.10, s32[1024]{0:T(1024)S(1)} %broadcast_clamp_fusion.1), kind=kCustom, calls=%fused_computation.12 | custom fusion | bytes 12288 | tf_op jit(solution)/shard_map/gather | solution.py:134
  244.2 4.4 %compare_select_fusion.6 = s32[1024,1]{0,1:T(1,128)S(1)} fusion(s32[]{:T(128)} %bitcast.9, s32[]{:T(128)} %bitcast.10, s32[]{:T(128)} %bitcast.11, s32[]{:T(128)} %bitcast.12, s32[]{:T(128)} %bitcast.13, s32[]{:T(128)} %bitcast.15, s32[]{:T(128)} %bitcast.14), kind=kLoop, calls=%fused_computation.38 | loop fusion | flops 23552 | bytes 4124 | tf_op jit(solution)/shard_map/gather | solution.py:126
  248.6 11.5 %all-to-all-done.1 = f32[8,1,34816]{2,1,0:T(1,128)S(1)} async-done(((f32[8,1,34816]{2,1,0:T(1,128)}), f32[8,1,34816]{2,1,0:T(1,128)S(1)}, u32[]{:S(2)}, u32[]{:S(2)}) %all-to-all-start.1) | async-done | bytes 1114144 | tf_op jit(solution)/shard_map/all_to_all | solution.py:33
  260.1 0.8 reduce_sum.19
  261.0 4.5 %gather_fusion.2 = f32[1024]{0:T(1024)S(1)} fusion(f32[1024]{0:T(1024)S(1)} %slice.224, s32[1024]{0:T(1024)S(1)} %get-tuple-element.19), kind=kCustom, calls=%fused_computation.2 | custom fusion | bytes 12288 | tf_op jit(solution)/shard_map/gather | solution.py:123
  265.5 4.5 %gather_fusion.3 = f32[1024]{0:T(1024)S(1)} fusion(f32[1024]{0:T(1024)S(1)} %get-tuple-element.5, s32[1024]{0:T(1024)S(1)} %get-tuple-element.19), kind=kCustom, calls=%fused_computation.3 | custom fusion | bytes 12288 | tf_op jit(solution)/shard_map/gather | solution.py:133
  270.1 4.5 %gather_fusion.5 = f32[1024]{0:T(1024)S(1)} fusion(f32[1024]{0:T(1024)S(1)} %min.46, s32[1024]{0:T(1024)S(1)} %broadcast_clamp_fusion.4), kind=kCustom, calls=%fused_computation.5 | custom fusion | bytes 12288 | tf_op jit(solution)/shard_map/gather | solution.py:133
  274.7 4.5 %gather_fusion.7 = f32[1024]{0:T(1024)S(1)} fusion(f32[1024]{0:T(1024)S(1)} %min.47, s32[1024]{0:T(1024)S(1)} %broadcast_clamp_fusion.3), kind=kCustom, calls=%fused_computation.7 | custom fusion | bytes 12288 | tf_op jit(solution)/shard_map/gather | solution.py:133
  279.2 4.5 %gather_fusion.9 = f32[1024]{0:T(1024)S(1)} fusion(f32[1024]{0:T(1024)S(1)} %min.48, s32[1024]{0:T(1024)S(1)} %broadcast_clamp_fusion.2), kind=kCustom, calls=%fused_computation.9 | custom fusion | bytes 12288 | tf_op jit(solution)/shard_map/gather | solution.py:133
  283.8 4.5 %gather_fusion.11 = f32[1024]{0:T(1024)S(1)} fusion(f32[1024]{0:T(1024)S(1)} %min.49, s32[1024]{0:T(1024)S(1)} %broadcast_clamp_fusion.1), kind=kCustom, calls=%fused_computation.11 | custom fusion | bytes 12288 | tf_op jit(solution)/shard_map/gather | solution.py:133
  288.3 4.5 %gather_fusion.13 = f32[1024]{0:T(1024)S(1)} fusion(f32[1024]{0:T(1024)S(1)} %min.50, s32[1024]{0:T(1024)S(1)} %broadcast_clamp_fusion), kind=kCustom, calls=%fused_computation.13 | custom fusion | bytes 12288 | tf_op jit(solution)/shard_map/gather | solution.py:133
  292.8 5.7 %minimum_select_fusion = (f32[1024]{0:T(1024)S(1)}, pred[1024]{0:T(1024)(128)(4,1)S(1)}) fusion(f32[1024]{0:T(1024)S(1)} %min.50, f32[1024]{0:T(1024)S(1)} %gather_fusion.13, pred[1024]{0:T(1024)(128)(4,1)S(1)} %get-tuple-element.7, pred[1024]{0:T(1024)(128)(4,1)S(1)} %compare_reduce_fusion, pred[1024]{0:T(1024)(128)(4,1)S(1)} %compare_reduce_fusion.1, ...), kind=kLoop, calls=%fused_computation.66 | loop fusion | flops 20480 | bytes 27684 | tf_op jit(solution)/shard_map/jit(_where)/select_n | solution.py:135
  300.4 0.7 broadcast_subtract_fusion
  (110 shorter events, 5.6 us)
Async XLA Ops:
  7.2 50.7 %all-gather.4.cloned.1.call-start = ((), (), s32[]{:S(2)}) async-start(), calls=%async_computation.3 | async-start | bytes 2621440 | tf_op jit(solution)/shard_map/all_gather | solution.py:20
  20.5 59.1 %all-gather.6.cloned.1.call-start = ((), (), s32[]{:S(2)}) async-start(), calls=%async_computation.4 | async-start | bytes 6291456 | tf_op jit(solution)/shard_map/all_gather | solution.py:20
  57.9 133.0 %reduce-scatter.2.cloned.1.call-start = ((), (), s32[]{:S(2)}) async-start(), calls=%async_computation.5 | async-start | bytes 9437184 | tf_op jit(solution)/shard_map/reduce_scatter | solution.py:96
  79.6 4.6 %copy-start.8 = (bf16[2048,2048]{1,0:T(8,128)(2,1)S(1)}, bf16[2048,2048]{1,0:T(8,128)(2,1)}, u32[]{:S(2)}) copy-start(bf16[2048,2048]{1,0:T(8,128)(2,1)} %param.9) | copy-start | bytes 25165828
  95.3 0.7 copy-start
  95.3 0.7 copy-start.4
  95.3 5.2 %copy-start.7 = (s32[16]{0:T(128)S(1)}, s32[16]{0:T(128)}, u32[]{:S(2)}) copy-start(s32[16]{0:T(128)} %param.15) | copy-start | bytes 196
  190.9 3.0 copy-start.1
  203.4 19.2 %all-to-all-start = ((f32[32,3,1024]{2,1,0:T(4,128)}), f32[32,3,1024]{2,1,0:T(4,128)S(1)}, u32[]{:S(2)}, u32[]{:S(2)}) async-start(f32[32,3,1024]{2,1,0:T(4,128)} %broadcast_in_dim.66), calls=%async_computation.1 | async-start | bytes 1048576 | tf_op jit(solution)/shard_map/all_to_all | solution.py:33
  225.4 34.8 %all-to-all-start.1 = ((f32[8,1,34816]{2,1,0:T(1,128)}), f32[8,1,34816]{2,1,0:T(1,128)S(1)}, u32[]{:S(2)}, u32[]{:S(2)}) async-start(f32[8,1,34816]{2,1,0:T(1,128)} %broadcast_in_dim.70), calls=%async_computation.2 | async-start | bytes 2228224 | tf_op jit(solution)/shard_map/all_to_all | solution.py:33
  234.0 9.5 %copy-start.3 = (s32[16]{0:T(128)S(1)}, s32[16]{0:T(128)}, u32[]{:S(2)}) copy-start(s32[16]{0:T(128)} %param.14) | copy-start | bytes 196
  238.6 26.9 %copy-start.5 = (f32[1024]{0:T(1024)S(1)}, f32[1024]{0:T(1024)}, u32[]{:S(2)}) copy-start(f32[1024]{0:T(1024)} %param.13) | copy-start | bytes 12292
  238.6 26.9 %copy-start.6 = (f32[1024]{0:T(1024)S(1)}, f32[1024]{0:T(1024)}, u32[]{:S(2)}) copy-start(f32[1024]{0:T(1024)} %param.12) | copy-start | bytes 12292
  260.9 9.1 %copy-start.2 = (f32[34816]{0:T(1024)}, f32[34816]{0:T(1024)S(1)}, u32[]{:S(2)}) copy-start(f32[34816]{0:T(1024)S(1)} %reduce_sum.19) | copy-start | bytes 417796
  283.7 16.0 %slice-start = ((f32[34816]{0:T(1024)}), f32[32768]{0:T(1024)S(1)}, s32[]{:S(2)}) async-start(f32[34816]{0:T(1024)} %copy-done.2), calls=%async_computation.6 | async-start | bytes 262144 | tf_op jit(solution)/shard_map/slice | solution.py:75
Sparse Core Ops, SparseCore 0:
  20.6 37.1 all-gather.3
  59.7 19.9 all-gather.5
  95.4 95.4 reduce-scatter.1
where the time goes:
time: 308 us
  waiting for transfers between devices  167 us (54%)
  local copies, waits for them, and re-layouts  74.7 us (24%)
  other arithmetic  15.4 us (5%)
  between operations  14.3 us (5%)
  blocking collectives  13.3 us (4%)
  starting transfers between devices  11.8 us (4%)
  matrix products  11 us (4%)
    reduce_scatter x1, waiting for transfers between devices, local(): lax.psum_scatter(jnp.dot(columns, lm_head, preferred_element_type=jnp.flo...  90.3 us
    all_gather x2, waiting for transfers between devices, all_blocks(): tiles = lax.all_gather(tiles, axes[k], axis=0, tiled=True)  59 us
    gather x6, local copies, waits for them, and re-layouts, local(): path_min = jnp.minimum(path_min, path_min[ancestor])  27.2 us
    gather x5, local copies, waits for them, and re-layouts, local(): ancestor = ancestor[ancestor]  22.6 us
    all_to_all x2, waiting for transfers between devices, from_everyone(): return lax.all_to_all(copies, axis, split_axis=0, concat_axis=0, tiled=True)  17.8 us
    all_gather x1, blocking collectives, all_blocks(): tiles = lax.all_gather(tiles, axes[k], axis=0, tiled=True)  13.3 us
    all_to_all x2, starting transfers between devices, from_everyone(): return lax.all_to_all(copies, axis, split_axis=0, concat_axis=0, tiled=True)  11.7 us
    dot_general x1, matrix products, local(): jnp.dot(columns, lm_head, preferred_element_type=jnp.float32)  11 us
  transfers between devices with their start and end apart: 5, of which 5 were waited for; matrix products, arithmetic and copies ran while one was open for 9% of the time, Pallas kernels for 0%

commit v1 on v0

--- a/solution.py
+++ b/solution.py
@@ -17,7 +17,9 @@
 def all_blocks(x, axes, sequence):
     tiles = x[None]
     for k in sequence:
-        tiles = lax.all_gather(tiles, axes[k], axis=0, tiled=True)
+        tiles = jnp.concatenate(
+            lax.all_to_all(jnp.stack([tiles] * lax.axis_size(axes[k])), axes[k], 0, 0), axis=0
+        )
     held = [lax.axis_size(axes[k]) for k in reversed(sequence)]
     tiles = tiles.reshape(*held, *x.shape)
     turned = sorted(range(len(sequence)), key=lambda place: sequence[len(sequence) - 1 - place])

time: 308 us -> 285 us (0.925)
  waiting for transfers between devices: 167 us -> 106 us
  blocking collectives: 13.3 us -> 51.5 us
    all_gather x2 -> x0, waiting for transfers between devices: 59 us -> none  [all_blocks(): tiles = lax.all_gather(tiles, axes[k], axis=0, tiled=True)]
    all_to_all x0 -> x3, blocking collectives: none -> 51.5 us  [all_blocks(): lax.all_to_all(jnp.stack([tiles] * lax.axis_size(axes[k])), axes[k], 0, 0)]
    all_gather x1 -> x0, blocking collectives: 13.3 us -> none  [all_blocks(): tiles = lax.all_gather(tiles, axes[k], axis=0, tiled=True)]
  transfers between devices with their start and end apart: 5 -> 3, of which waited for: 5 -> 3; matrix products, arithmetic and copies ran while one was open for 9% -> 10% of each run, Pallas kernels for 0% -> 0%
where the time goes in v1:
time: 285 us; the launch traced here: 284 us
  waiting for transfers between devices  106 us (37%)
  local copies, waits for them, and re-layouts  73.5 us (26%)
  blocking collectives  51.5 us (18%)
  other arithmetic  15.8 us (6%)
  between operations  14.7 us (5%)
  starting transfers between devices  11.7 us (4%)
  matrix products  11 us (4%)
    reduce_scatter x1, waiting for transfers between devices, local(): lax.psum_scatter(jnp.dot(columns, lm_head, preferred_element_type=jnp.flo...  88.5 us
    all_to_all x3, blocking collectives, all_blocks(): lax.all_to_all(jnp.stack([tiles] * lax.axis_size(axes[k])), axes[k], 0, 0)  51.5 us
    gather x6, local copies, waits for them, and re-layouts, local(): path_min = jnp.minimum(path_min, path_min[ancestor])  27.2 us
    gather x5, local copies, waits for them, and re-layouts, local(): ancestor = ancestor[ancestor]  22.6 us
    all_to_all x2, waiting for transfers between devices, from_everyone(): return lax.all_to_all(copies, axis, split_axis=0, concat_axis=0, tiled=True)  17.8 us
    all_to_all x2, starting transfers between devices, from_everyone(): return lax.all_to_all(copies, axis, split_axis=0, concat_axis=0, tiled=True)  11.7 us
    dot_general x1, matrix products, local(): jnp.dot(columns, lm_head, preferred_element_type=jnp.float32)  11 us
    gather x1, local copies, waits for them, and re-layouts, local(): emitted_scores[jnp.clip(own_parent, 0, row_count - 1), jnp.clip(own_token...  8.59 us
  transfers between devices with their start and end apart: 3, of which 3 were waited for; matrix products, arithmetic and copies ran while one was open for 10% of the time, Pallas kernels for 0%

profile of v1, /device:TPU:1, one launch (start us, length us, event | category | flops | bytes accessed | tf_op | source)
XLA Modules:
  0.0 284.4 jit_solution(3016915245369915493)
XLA Ops:
  7.2 0.9 stack.9
  8.2 13.4 %all_to_all.26 = bf16[4,1,32,2048]{3,2,1,0:T(8,128)(2,1)S(1)} all-to-all(bf16[4,1,32,2048]{3,2,1,0:T(8,128)(2,1)S(1)} %stack.9), channel_id=1, replica_groups=mesh['gx_0'=4,'gx_1'=4,'gx_2'=2,'gy'=8] {'gx_1'}, dimensions={0} | all-to-all | bytes 1048576 | tf_op jit(solution)/shard_map/all_to_all | solution.py:21
  21.8 27.9 %all_to_all.27 = bf16[4,4,32,2048]{3,2,1,0:T(8,128)(2,1)S(1)} all-to-all(bf16[4,4,32,2048]{3,2,1,0:T(8,128)(2,1)S(1)} %stack.10), channel_id=1, replica_groups=mesh['gx_0'=4,'gx_1'=4,'gx_2'=2,'gy'=8] {'gx_0'}, dimensions={0} | all-to-all | bytes 4194304 | tf_op jit(solution)/shard_map/all_to_all | solution.py:21
  50.1 10.2 %all_to_all.28 = bf16[2,16,32,2048]{3,2,1,0:T(8,128)(2,1)S(1)} all-to-all(bf16[2,16,32,2048]{3,2,1,0:T(8,128)(2,1)S(1)} %pad_maximum_fusion), channel_id=1, replica_groups=mesh['gx_0'=4,'gx_1'=4,'gx_2'=2,'gy'=8] {'gx_2'}, dimensions={0} | all-to-all | bytes 8388608 | tf_op jit(solution)/shard_map/all_to_all | solution.py:21
  60.9 1.6 slice-done.2
  62.5 11.0 %fusion.17 = f32[1024,2048]{1,0:T(8,128)} fusion(bf16[1024,2048]{1,0:T(8,128)(2,1)S(1)} %bitcast.57, bf16[2048,2048]{1,0:T(8,128)(2,1)S(1)} %bitcast.73), kind=kOutput, calls=%fused_computation.95 | convolution fusion | flops 8589934592 | bytes 20971520 | tf_op jit(solution)/shard_map/dot_general | solution.py:99
  74.2 4.5 %gather_fusion.4 = s32[1024]{0:T(1024)S(1)} fusion(s32[1024]{0:T(1024)S(1)} %copy-done, s32[1024]{0:T(1024)S(1)} %get-tuple-element.19), kind=kCustom, calls=%fused_computation.4 | custom fusion | bytes 12288 | tf_op jit(solution)/shard_map/gather | solution.py:136
  78.8 88.5 %reduce-scatter.2.cloned.1.call-done = f32[128,2048]{1,0:T(8,128)} async-done(((f32[1024,2048]{1,0:T(8,128)}), f32[128,2048]{1,0:T(8,128)}) %reduce-scatter.2.cloned.1.call-update) | async-done | bytes 1048592 | tf_op jit(solution)/shard_map/reduce_scatter | solution.py:98
  167.3 1.4 reduce_max.9
  168.8 1.5 exponential_reduce_fusion
  170.3 8.6 %gather_fusion = f32[1024]{0:T(1024)S(1)} fusion(f32[128,2048]{1,0:T(8,128)S(1)} %copy-done.1, s32[1024]{0:T(1024)S(1)} %get-tuple-element.20), kind=kCustom, calls=%fused_computation | custom fusion | bytes 16384 | tf_op jit(solution)/shard_map/gather | solution.py:107
  178.9 0.9 broadcast_in_dim.62
  179.9 7.6 %all-to-all-start.3 = ((f32[32,3,1024]{2,1,0:T(4,128)}), f32[32,3,1024]{2,1,0:T(4,128)S(1)}, u32[]{:S(2)}, u32[]{:S(2)}) async-start(f32[32,3,1024]{2,1,0:T(4,128)} %broadcast_in_dim.62), calls=%async_computation.4 | async-start | bytes 1048576 | tf_op jit(solution)/shard_map/all_to_all | solution.py:35
  187.5 4.5 %gather_fusion.6 = s32[1024]{0:T(1024)S(1)} fusion(s32[1024]{0:T(1024)S(1)} %gather_fusion.4, s32[1024]{0:T(1024)S(1)} %broadcast_clamp_fusion.4), kind=kCustom, calls=%fused_computation.6 | custom fusion | bytes 12288 | tf_op jit(solution)/shard_map/gather | solution.py:136
  192.7 6.3 %all-to-all-done.3 = f32[32,3,1024]{2,1,0:T(4,128)S(1)} async-done(((f32[32,3,1024]{2,1,0:T(4,128)}), f32[32,3,1024]{2,1,0:T(4,128)S(1)}, u32[]{:S(2)}, u32[]{:S(2)}) %all-to-all-start.3) | async-done | bytes 393248 | tf_op jit(solution)/shard_map/all_to_all | solution.py:35
  200.2 1.6 broadcast_in_dim.66
  201.8 4.1 %all-to-all-start.4 = ((f32[8,1,34816]{2,1,0:T(1,128)}), f32[8,1,34816]{2,1,0:T(1,128)S(1)}, u32[]{:S(2)}, u32[]{:S(2)}) async-start(f32[8,1,34816]{2,1,0:T(1,128)} %broadcast_in_dim.66), calls=%async_computation.5 | async-start | bytes 2228224 | tf_op jit(solution)/shard_map/all_to_all | solution.py:35
  205.9 4.5 %gather_fusion.8 = s32[1024]{0:T(1024)S(1)} fusion(s32[1024]{0:T(1024)S(1)} %gather_fusion.6, s32[1024]{0:T(1024)S(1)} %broadcast_clamp_fusion.3), kind=kCustom, calls=%fused_computation.8 | custom fusion | bytes 12288 | tf_op jit(solution)/shard_map/gather | solution.py:136
  210.5 4.5 %gather_fusion.10 = s32[1024]{0:T(1024)S(1)} fusion(s32[1024]{0:T(1024)S(1)} %gather_fusion.8, s32[1024]{0:T(1024)S(1)} %broadcast_clamp_fusion.2), kind=kCustom, calls=%fused_computation.10 | custom fusion | bytes 12288 | tf_op jit(solution)/shard_map/gather | solution.py:136
  215.1 4.5 %gather_fusion.12 = s32[1024]{0:T(1024)S(1)} fusion(s32[1024]{0:T(1024)S(1)} %gather_fusion.10, s32[1024]{0:T(1024)S(1)} %broadcast_clamp_fusion.1), kind=kCustom, calls=%fused_computation.12 | custom fusion | bytes 12288 | tf_op jit(solution)/shard_map/gather | solution.py:136
  220.6 4.4 %compare_select_fusion.6 = s32[1024,1]{0,1:T(1,128)S(1)} fusion(s32[]{:T(128)} %bitcast.9, s32[]{:T(128)} %bitcast.10, s32[]{:T(128)} %bitcast.11, s32[]{:T(128)} %bitcast.12, s32[]{:T(128)} %bitcast.13, s32[]{:T(128)} %bitcast.15, s32[]{:T(128)} %bitcast.14), kind=kLoop, calls=%fused_computation.39 | loop fusion | flops 23552 | bytes 4124 | tf_op jit(solution)/shard_map/gather | solution.py:128
  225.0 11.5 %all-to-all-done.4 = f32[8,1,34816]{2,1,0:T(1,128)S(1)} async-done(((f32[8,1,34816]{2,1,0:T(1,128)}), f32[8,1,34816]{2,1,0:T(1,128)S(1)}, u32[]{:S(2)}, u32[]{:S(2)}) %all-to-all-start.4) | async-done | bytes 1114144 | tf_op jit(solution)/shard_map/all_to_all | solution.py:35
  236.6 0.8 reduce_sum.19
  237.4 4.5 %gather_fusion.2 = f32[1024]{0:T(1024)S(1)} fusion(f32[1024]{0:T(1024)S(1)} %slice.224, s32[1024]{0:T(1024)S(1)} %get-tuple-element.19), kind=kCustom, calls=%fused_computation.2 | custom fusion | bytes 12288 | tf_op jit(solution)/shard_map/gather | solution.py:125
  242.0 4.5 %gather_fusion.3 = f32[1024]{0:T(1024)S(1)} fusion(f32[1024]{0:T(1024)S(1)} %get-tuple-element.5, s32[1024]{0:T(1024)S(1)} %get-tuple-element.19), kind=kCustom, calls=%fused_computation.3 | custom fusion | bytes 12288 | tf_op jit(solution)/shard_map/gather | solution.py:135
  246.5 4.5 %gather_fusion.5 = f32[1024]{0:T(1024)S(1)} fusion(f32[1024]{0:T(1024)S(1)} %min.46, s32[1024]{0:T(1024)S(1)} %broadcast_clamp_fusion.4), kind=kCustom, calls=%fused_computation.5 | custom fusion | bytes 12288 | tf_op jit(solution)/shard_map/gather | solution.py:135
  251.1 4.5 %gather_fusion.7 = f32[1024]{0:T(1024)S(1)} fusion(f32[1024]{0:T(1024)S(1)} %min.47, s32[1024]{0:T(1024)S(1)} %broadcast_clamp_fusion.3), kind=kCustom, calls=%fused_computation.7 | custom fusion | bytes 12288 | tf_op jit(solution)/shard_map/gather | solution.py:135
  255.6 4.5 %gather_fusion.9 = f32[1024]{0:T(1024)S(1)} fusion(f32[1024]{0:T(1024)S(1)} %min.48, s32[1024]{0:T(1024)S(1)} %broadcast_clamp_fusion.2), kind=kCustom, calls=%fused_computation.9 | custom fusion | bytes 12288 | tf_op jit(solution)/shard_map/gather | solution.py:135
  260.2 4.5 %gather_fusion.11 = f32[1024]{0:T(1024)S(1)} fusion(f32[1024]{0:T(1024)S(1)} %min.49, s32[1024]{0:T(1024)S(1)} %broadcast_clamp_fusion.1), kind=kCustom, calls=%fused_computation.11 | custom fusion | bytes 12288 | tf_op jit(solution)/shard_map/gather | solution.py:135
  264.7 4.5 %gather_fusion.13 = f32[1024]{0:T(1024)S(1)} fusion(f32[1024]{0:T(1024)S(1)} %min.50, s32[1024]{0:T(1024)S(1)} %broadcast_clamp_fusion), kind=kCustom, calls=%fused_computation.13 | custom fusion | bytes 12288 | tf_op jit(solution)/shard_map/gather | solution.py:135
  269.3 5.7 %minimum_select_fusion = (f32[1024]{0:T(1024)S(1)}, pred[1024]{0:T(1024)(128)(4,1)S(1)}) fusion(f32[1024]{0:T(1024)S(1)} %min.50, f32[1024]{0:T(1024)S(1)} %gather_fusion.13, pred[1024]{0:T(1024)(128)(4,1)S(1)} %get-tuple-element.7, pred[1024]{0:T(1024)(128)(4,1)S(1)} %compare_reduce_fusion, pred[1024]{0:T(1024)(128)(4,1)S(1)} %compare_reduce_fusion.1, ...), kind=kLoop, calls=%fused_computation.67 | loop fusion | flops 20480 | bytes 27684 | tf_op jit(solution)/shard_map/jit(_where)/select_n | solution.py:137
  276.8 0.7 broadcast_subtract_fusion
  (112 shorter events, 6.7 us)
Async XLA Ops:
  7.2 160.1 %reduce-scatter.2.cloned.1.call-start = ((), (), s32[]{:S(2)}) async-start(), calls=%async_computation.6 | async-start | bytes 9437184 | tf_op jit(solution)/shard_map/reduce_scatter | solution.py:98
  50.1 10.8 %slice-start.1 = ((s8[8388608]{0:T(1024)(128)(4,1)}), s8[4194304]{0:T(1024)(128)(4,1)S(1)}, s32[]{:S(2)}) async-start(s8[8388608]{0:T(1024)(128)(4,1)} %bitcast.72), calls=%async_computation.8 | async-start | bytes 8388608
  60.3 2.2 slice-start.2
  73.5 0.7 copy-start
  73.5 0.7 copy-start.4
  73.5 5.2 %copy-start.7 = (s32[16]{0:T(128)S(1)}, s32[16]{0:T(128)}, u32[]{:S(2)}) copy-start(s32[16]{0:T(128)} %param.15) | copy-start | bytes 196
  167.3 3.0 %copy-start.1 = (f32[128,2048]{1,0:T(8,128)S(1)}, f32[128,2048]{1,0:T(8,128)}, u32[]{:S(2)}) copy-start(f32[128,2048]{1,0:T(8,128)} %reduce-scatter.2.cloned.1.call-done) | copy-start | bytes 3145732
  179.9 19.2 %all-to-all-start.3 = ((f32[32,3,1024]{2,1,0:T(4,128)}), f32[32,3,1024]{2,1,0:T(4,128)S(1)}, u32[]{:S(2)}, u32[]{:S(2)}) async-start(f32[32,3,1024]{2,1,0:T(4,128)} %broadcast_in_dim.62), calls=%async_computation.4 | async-start | bytes 1048576 | tf_op jit(solution)/shard_map/all_to_all | solution.py:35
  201.8 34.8 %all-to-all-start.4 = ((f32[8,1,34816]{2,1,0:T(1,128)}), f32[8,1,34816]{2,1,0:T(1,128)S(1)}, u32[]{:S(2)}, u32[]{:S(2)}) async-start(f32[8,1,34816]{2,1,0:T(1,128)} %broadcast_in_dim.66), calls=%async_computation.5 | async-start | bytes 2228224 | tf_op jit(solution)/shard_map/all_to_all | solution.py:35
  210.5 9.5 %copy-start.3 = (s32[16]{0:T(128)S(1)}, s32[16]{0:T(128)}, u32[]{:S(2)}) copy-start(s32[16]{0:T(128)} %param.14) | copy-start | bytes 196
  215.0 26.9 %copy-start.5 = (f32[1024]{0:T(1024)S(1)}, f32[1024]{0:T(1024)}, u32[]{:S(2)}) copy-start(f32[1024]{0:T(1024)} %param.13) | copy-start | bytes 12292
  215.0 26.9 %copy-start.6 = (f32[1024]{0:T(1024)S(1)}, f32[1024]{0:T(1024)}, u32[]{:S(2)}) copy-start(f32[1024]{0:T(1024)} %param.12) | copy-start | bytes 12292
  237.4 9.1 %copy-start.2 = (f32[34816]{0:T(1024)}, f32[34816]{0:T(1024)S(1)}, u32[]{:S(2)}) copy-start(f32[34816]{0:T(1024)S(1)} %reduce_sum.19) | copy-start | bytes 417796
  260.2 16.0 %slice-start = ((f32[34816]{0:T(1024)}), f32[32768]{0:T(1024)S(1)}, s32[]{:S(2)}) async-start(f32[34816]{0:T(1024)} %copy-done.2), calls=%async_computation.7 | async-start | bytes 262144 | tf_op jit(solution)/shard_map/slice | solution.py:77
Sparse Core Ops, SparseCore 0:
  73.6 93.6 reduce-scatter.1
